TPU v7x, 256 devices: a whole 4x4x8 slice. The times are simulated.
256 devices in a mesh: ctx: 32 (over z_lo, x, y), tp: 8 (over z_hi, core).
Axes of the slice: x: 4, y: 4, z: 8 (z_hi: 4, z_lo: 2; z = z_hi * 2 + z_lo), core: 2. Of those that a mesh axis runs over, the one named last changes fastest.
Arguments:
- queries: bfloat16 [4096, 8192], P('ctx', 'tp'), may hold values from -8 to 8
- span_kv: bfloat16 [4096, 8, 2, 128], P('ctx', 'tp'), may hold values from -8 to 8
- cache_kv: bfloat16 [16384, 8, 2, 128], P('ctx', 'tp'), may hold values from -4 to 4
- out_weight: bfloat16 [8192, 8192], P('tp', 'ctx'), may hold values from -2.390625 to 2.390625
- offset: int32 [1], replicated, may hold values from 16384 to 24575
- lengths: int32 [64], replicated, may hold values from 64 to 256, as said below
Outputs:
- mixed: bfloat16 [4096, 8192], P('tp', 'ctx')
Inputs may be any that keep to these rules, and one draw needn't show every extreme that they name: `lengths`: each at most 256; in every draw some match has all 256 of its positions valid.
All inputs are finite; a program needn't handle non-finite values.
Results may differ from a plain program's by a relative error of at most 0.025.
Values may be sent and summed in bfloat16 or wider, within the bound.
A program may use at most 64 MiB of HBM per device.

v0:
```python
import math
import jax
import jax.numpy as jnp
from jax import lax
from jax.sharding import PartitionSpec as P

SLOT = 256
lowest_score = -1e30
rope_base = 500000.0


def rotate(values, positions):
    head_size = values.shape[-1]
    half_dim = head_size // 2
    frequency = jnp.exp(
        jnp.arange(half_dim, dtype=jnp.float32) * (-2.0 * math.log(rope_base) / head_size)
    )
    angles = positions.astype(jnp.float32)[:, None] * frequency[None, :]
    cosine = jnp.cos(angles)[:, None, :]
    sine_part = jnp.sin(angles)[:, None, :]
    first_half = values[..., :half_dim]
    second_half = values[..., half_dim:]
    return jnp.concatenate(
        [
            first_half * cosine - second_half * sine_part,
            second_half * cosine + first_half * sine_part,
        ],
        axis=-1,
    )


def key_block(count):
    for option in (2048, 1536, 1024, 768, 512, 384, 256, 128):
        return option
    return count


def slot_valid(cache_positions, lengths):
    match_ids = jnp.arange(lengths.shape[0], dtype=jnp.int32)
    owner = cache_positions // SLOT
    limit = jnp.sum(jnp.where(owner[:, None] == match_ids[None, :], lengths[None, :], 0), axis=1)
    return cache_positions % SLOT < limit


def online_update(carry_state, grouped, key_rows, value_rows, valid, scale):
    running_max, running_sum, accum = carry_state
    scores = (
        jnp.einsum("tkgd,nkd->tkgn", grouped, key_rows, preferred_element_type=jnp.float32) * scale
    )
    scores = jnp.where(valid, scores, lowest_score)
    new_max = jnp.maximum(running_max, jnp.max(scores, axis=-1))
    factor = jnp.exp(running_max - new_max)
    weights = jnp.where(valid, jnp.exp(scores - new_max[..., None]), 0.0)
    running_sum = running_sum * factor + jnp.sum(weights, axis=-1)
    update = jnp.einsum(
        "tkgn,nkd->tkgd",
        weights.astype(jnp.bfloat16),
        value_rows,
        preferred_element_type=jnp.float32,
    )
    accum = accum * factor[..., None] + update
    return (new_max, running_sum, accum)


def fold_blocks(carry_state, grouped, piece, mask_rule, scale):
    count = piece.shape[0]
    block = key_block(count)
    block_count = count // block
    kv_local = piece.shape[1]
    head_size = piece.shape[3]
    key_rows = piece[:, :, 0, :].reshape(block_count, block, kv_local, head_size)
    value_rows = piece[:, :, 1, :].reshape(block_count, block, kv_local, head_size)

    def advance(state_now, inputs):
        block_keys, block_values, index = inputs
        positions = index * block + jnp.arange(block, dtype=jnp.int32)
        valid = mask_rule(positions)
        return (online_update(state_now, grouped, block_keys, block_values, valid, scale), None)

    result, unused = lax.scan(
        advance, carry_state, (key_rows, value_rows, jnp.arange(block_count, dtype=jnp.int32))
    )
    return result


def body(queries, span_kv, cache_kv, out_weight, offset, lengths):
    tok_rows, width = queries.shape
    kv_local = span_kv.shape[1]
    head_size = span_kv.shape[3]
    heads_local = width // head_size
    group = heads_local // kv_local
    scale = 1.0 / math.sqrt(head_size)
    ctx_index = lax.axis_index("ctx")
    first_token = ctx_index * tok_rows
    token_ids = first_token + jnp.arange(tok_rows, dtype=jnp.int32)
    positions = offset[0] + token_ids
    rotated = rotate(
        queries.reshape(tok_rows, heads_local, head_size).astype(jnp.float32), positions
    ).astype(jnp.bfloat16)
    grouped = rotated.reshape(tok_rows, kv_local, group, head_size)
    span_keys = rotate(span_kv[:, :, 0, :].astype(jnp.float32), positions).astype(jnp.bfloat16)
    span_rotated = jnp.stack([span_keys, span_kv[:, :, 1, :]], axis=2)

    def cache_rule(key_positions):
        return slot_valid(key_positions, lengths)[None, None, None, :]

    def span_rule(key_positions):
        return (key_positions[None, :] <= token_ids[:, None])[:, None, None, :]

    start_state = (
        jnp.full((tok_rows, kv_local, group), lowest_score, jnp.float32),
        jnp.zeros((tok_rows, kv_local, group), jnp.float32),
        jnp.zeros((tok_rows, kv_local, group, head_size), jnp.float32),
    )
    state_now = fold_blocks(
        start_state, grouped, lax.all_gather(cache_kv, "ctx", axis=0, tiled=True), cache_rule, scale
    )
    state_now = fold_blocks(
        state_now,
        grouped,
        lax.all_gather(span_rotated, "ctx", axis=0, tiled=True),
        span_rule,
        scale,
    )
    attention = (state_now[2] / state_now[1][..., None]).astype(jnp.bfloat16)
    attention = attention.reshape(tok_rows, heads_local * head_size)
    projected = jnp.dot(
        lax.all_gather(attention, "ctx", axis=0, tiled=True),
        out_weight,
        preferred_element_type=jnp.float32,
    )
    return lax.psum_scatter(projected.astype(jnp.bfloat16), "tp", scatter_dimension=0, tiled=True)


def solution(mesh):
    return jax.shard_map(
        body,
        mesh=mesh,
        in_specs=(
            P("ctx", "tp"),
            P("ctx", "tp", None, None),
            P("ctx", "tp", None, None),
            P("tp", "ctx"),
            P(),
            P(),
        ),
        out_specs=P("tp", "ctx"),
        check_vma=False,
    )
```

profile of v0, /device:TPU:16, one launch (start us, length us, event | category | flops | bytes accessed | tf_op | source)
XLA Modules:
  0.0 690.7 jit_solution(2015191303401559980)
XLA Ops:
  7.3 1.0 fusion.74
  9.5 1.7 copy.27
  11.3 1.1 copy.28
  12.9 125.5 %all-gather.6.cloned.1.call-done = bf16[4096,1,2,128]{0,3,2,1:T(8,128)(2,1)} async-done(((bf16[128,1,2,128]{0,3,2,1:T(8,128)(2,1)}), bf16[4096,1,2,128]{0,3,2,1:T(8,128)(2,1)}) %all-gather.6.cloned.1.call-update) | async-done | bytes 2097168 | tf_op jit(solution)/shard_map/all_gather | solution.py:121
  138.4 2.7 fusion.73
  141.1 1.6 copy.34
  142.8 1.3 copy.35
  144.1 162.4 %all-gather.4.cloned.1.call-done = bf16[16384,1,2,128]{3,0,2,1:T(8,128)(2,1)} async-done(((bf16[512,1,2,128]{3,0,2,1:T(8,128)(2,1)}), bf16[16384,1,2,128]{3,0,2,1:T(8,128)(2,1)}) %all-gather.4.cloned.1.call-update) | async-done | bytes 8388624 | tf_op jit(solution)/shard_map/all_gather | solution.py:116
  306.5 5.7 fusion.72
  312.2 126.6 %while.33 = (s32[]{:T(128)}, f32[128,1,8]{0,2,1:T(8,128)S(1)}, f32[128,1,8]{0,2,1:T(8,128)S(1)}, f32[128,1,8,128]{0,3,2,1:T(8,128)S(1)}, s32[8]{0:T(128)S(1)}, /...) while((s32[]{:T(128)}, f32[128,1,8]{0,2,1:T(8,128)S(1)}, ...), condition=%wide.region_4.5_spmd.clone, body=%wide.region_0.4_spmd.clone.sunk | while | flops 1101854720 | bytes 52800976 | solution.py:80
  313.6 5.6 bitcast_reduce_fusion.2
  319.2 5.2 fusion.100
  324.5 0.8 slice-done.1
  325.3 2.7 fusion.99
  329.4 5.6 bitcast_reduce_fusion.2
  335.1 5.2 fusion.100
  341.1 2.7 fusion.99
  345.3 5.6 bitcast_reduce_fusion.2
  350.9 5.2 fusion.100
  356.1 0.8 slice-done.1
  356.9 2.7 fusion.99
  361.1 5.6 bitcast_reduce_fusion.2
  366.7 5.2 fusion.100
  372.8 2.7 fusion.99
  376.9 5.6 bitcast_reduce_fusion.2
  382.5 5.2 fusion.100
  387.8 0.8 slice-done.1
  388.6 2.7 fusion.99
  392.8 5.6 bitcast_reduce_fusion.2
  398.4 5.2 fusion.100
  404.4 2.7 fusion.99
  408.6 5.6 bitcast_reduce_fusion.2
  414.2 5.2 fusion.100
  419.4 0.8 slice-done.1
  420.2 2.7 fusion.99
  424.4 5.6 bitcast_reduce_fusion.2
  430.0 5.2 fusion.100
  436.1 2.7 fusion.99
  438.8 14.6 %while.32 = (s32[]{:T(128)}, f32[128,1,8]{0,2,1:T(8,128)S(1)}, f32[128,1,8]{0,2,1:T(8,128)S(1)}, f32[128,1,8,128]{0,3,2,1:T(8,128)S(1)}, s32[2]{0:T(128)S(1)}, /...) while((s32[]{:T(128)}, f32[128,1,8]{0,2,1:T(8,128)S(1)}, ...), condition=%wide.region_8.9_spmd.clone, body=%wide.region_5.8_spmd.clone.sunk | while | flops 1101534336 | bytes 32851120 | solution.py:80
  440.4 1.4 fusion.91
  441.8 2.2 fusion.94
  444.0 2.0 fusion.93
  447.7 1.4 fusion.91
  449.1 2.2 fusion.94
  451.3 2.0 fusion.93
  454.4 178.3 %all-gather.8.cloned.1.call-done = bf16[4096,1024]{0,1:T(8,128)(2,1)} async-done(((bf16[128,1024]{0,1:T(8,128)(2,1)}), bf16[4096,1024]{0,1:T(8,128)(2,1)}) %all-gather.8.cloned.1.call-update) | async-done | bytes 8388624 | tf_op jit(solution)/shard_map/all_gather | solution.py:128
  632.7 7.2 %convolution_convert_fusion = bf16[4096,256]{1,0:T(8,128)(2,1)} fusion(bf16[4096,1024]{0,1:T(8,128)(2,1)} %all-gather.8.cloned.1.call-done, bf16[1024,256]{1,0:T(8,128)(2,1)S(1)} %copy-done), kind=kOutput, calls=%fused_computation.74 | convolution fusion | flops 2148532224 | bytes 11010048 | tf_op jit(solution)/shard_map/dot_general | solution.py:127
  639.9 44.3 %reduce-scatter.2.cloned.1.call-done = bf16[512,256]{1,0:T(8,128)(2,1)} async-done(((bf16[4096,256]{1,0:T(8,128)(2,1)}), bf16[512,256]{1,0:T(8,128)(2,1)}) %reduce-scatter.2.cloned.1.call-update) | async-done | bytes 262160 | tf_op jit(solution)/shard_map/reduce_scatter | solution.py:132
  (140 shorter events, 14.3 us)
Async XLA Ops:
  6.5 626.1 %copy-start = (bf16[1024,256]{1,0:T(8,128)(2,1)S(1)}, bf16[1024,256]{1,0:T(8,128)(2,1)}, u32[]{:S(2)}) copy-start(bf16[1024,256]{1,0:T(8,128)(2,1)} %param.13) | copy-start | bytes 1572868
  6.5 131.9 %all-gather.6.cloned.1.call-start = ((), (), s32[]{:S(2)}) async-start(), calls=%async_computation.2 | async-start | bytes 2162688 | tf_op jit(solution)/shard_map/all_gather | solution.py:121
  9.4 297.0 %all-gather.4.cloned.1.call-start = ((), (), s32[]{:S(2)}) async-start(), calls=%async_computation.1 | async-start | bytes 8650752 | tf_op jit(solution)/shard_map/all_gather | solution.py:116
  11.2 621.5 %all-gather.8.cloned.1.call-start = ((), (), s32[]{:S(2)}) async-start(), calls=%async_computation.3 | async-start | bytes 8650752 | tf_op jit(solution)/shard_map/all_gather | solution.py:128
  144.1 168.1 %copy-start.2 = (s32[64]{0:T(128)S(1)}, s32[64]{0:T(128)}, u32[]{:S(2)}) copy-start(s32[64]{0:T(128)} %param.15) | copy-start | bytes 772
  319.2 5.3 slice-start
  319.2 6.1 slice-start.1
  335.0 5.3 slice-start
  335.0 6.1 slice-start.1
  350.9 5.3 slice-start
  350.9 6.1 slice-start.1
  366.7 5.3 slice-start
  366.7 6.1 slice-start.1
  382.5 5.3 slice-start
  382.5 6.1 slice-start.1
  398.3 5.3 slice-start
  398.4 6.1 slice-start.1
  414.2 5.3 slice-start
  414.2 6.1 slice-start.1
  430.0 5.3 slice-start
  430.0 6.1 slice-start.1
  438.8 3.0 copy-start.1
  446.1 3.0 copy-start.1
  454.1 230.0 %reduce-scatter.2.cloned.1.call-start = ((), (), s32[]{:S(2)}) async-start(), calls=%async_computation.4 | async-start | bytes 2359296 | tf_op jit(solution)/shard_map/reduce_scatter | solution.py:132
Sparse Core Ops, SparseCore 0:
  9.6 128.8 all-gather.5
  140.2 166.1 all-gather.3
  454.3 178.3 all-gather.7
  640.0 44.1 reduce-scatter.1
where the time goes:
time: 691 us
  waiting for transfers between devices  510 us (74%)
  matrix products  101 us (15%)
  other arithmetic  29.7 us (4%)
  local copies, waits for them, and re-layouts  28 us (4%)
  between operations  14 us (2%)
  loops' own time  7.33 us (1%)
    all_gather x1, waiting for transfers between devices, body(): lax.all_gather(attention, 'ctx', axis=0, tiled=True)  178 us
    all_gather x1, waiting for transfers between devices, body(): lax.all_gather(cache_kv, 'ctx', axis=0, tiled=True)  162 us
    all_gather x1, waiting for transfers between devices, body(): lax.all_gather(span_rotated, 'ctx', axis=0, tiled=True)  125 us
    dot_general x10, matrix products, online_update(): jnp.einsum('tkgd,nkd->tkgn', grouped, key_rows, preferred_element_type=jn...  47.4 us
    dot_general x10, matrix products, online_update(): jnp.einsum('tkgn,nkd->tkgd', weights.astype(jnp.bfloat16), value_rows, pr...  46.3 us
    reduce_scatter x1, waiting for transfers between devices, body(): lax.psum_scatter(projected.astype(jnp.bfloat16), 'tp', scatter_dimension=...  44.3 us
    reduce_sum x10, other arithmetic, online_update(): running_sum = running_sum * factor + jnp.sum(weights, axis=-1)  25.3 us
  transfers between devices with their start and end apart: 4, of which 4 were waited for; matrix products, arithmetic and copies ran while one was open for 1% of the time, Pallas kernels for 0%

commit v1 on v0

--- a/solution.py
+++ b/solution.py
@@ -118,7 +118,9 @@
     state_now = fold_blocks(
         state_now,
         grouped,
-        lax.all_gather(span_rotated, "ctx", axis=0, tiled=True),
+        jnp.concatenate(
+            lax.all_to_all(jnp.stack([span_rotated] * lax.axis_size("ctx")), "ctx", 0, 0), axis=0
+        ),
         span_rule,
         scale,
     )

time: 691 us -> 582 us (0.84)
  waiting for transfers between devices: 510 us -> 395 us
  starting transfers between devices: 0.31 us -> 9.04 us
    all_gather x1 -> x0, waiting for transfers between devices: 125 us -> none  [body(): lax.all_gather(span_rotated, 'ctx', axis=0, tiled=True)]
    all_to_all x0 -> x1, waiting for transfers between devices: none -> 29.3 us  [body(): lax.all_to_all(jnp.stack([span_rotated] * lax.axis_size('ctx')), 'ctx', 0...]
    all_gather x1, waiting for transfers between devices: 162 us -> 146 us  [body(): lax.all_gather(cache_kv, 'ctx', axis=0, tiled=True)]
    all_to_all x0 -> x1, starting transfers between devices: none -> 8.77 us  [body(): lax.all_to_all(jnp.stack([span_rotated] * lax.axis_size('ctx')), 'ctx', 0...]
where the time goes in v1:
time: 582 us; the launch traced here: 581 us
  waiting for transfers between devices  395 us (68%)
  matrix products  101 us (17%)
  other arithmetic  29.1 us (5%)
  local copies, waits for them, and re-layouts  25.6 us (4%)
  between operations  13.9 us (2%)
  starting transfers between devices  9.04 us (2%)
  loops' own time  7.33 us (1%)
    all_gather x1, waiting for transfers between devices, body(): lax.all_gather(attention, 'ctx', axis=0, tiled=True)  175 us
    all_gather x1, waiting for transfers between devices, body(): lax.all_gather(cache_kv, 'ctx', axis=0, tiled=True)  146 us
    dot_general x10, matrix products, online_update(): jnp.einsum('tkgd,nkd->tkgn', grouped, key_rows, preferred_element_type=jn...  47.4 us
    dot_general x10, matrix products, online_update(): jnp.einsum('tkgn,nkd->tkgd', weights.astype(jnp.bfloat16), value_rows, pr...  46.3 us
    reduce_scatter x1, waiting for transfers between devices, body(): lax.psum_scatter(projected.astype(jnp.bfloat16), 'tp', scatter_dimension=...  43.9 us
    all_to_all x1, waiting for transfers between devices, body(): lax.all_to_all(jnp.stack([span_rotated] * lax.axis_size('ctx')), 'ctx', 0...  29.3 us
    reduce_sum x10, other arithmetic, online_update(): running_sum = running_sum * factor + jnp.sum(weights, axis=-1)  25.3 us
  transfers between devices with their start and end apart: 4, of which 4 were waited for; matrix products, arithmetic and copies ran while one was open for 1% of the time, Pallas kernels for 0%

profile of v1, /device:TPU:16, one launch (start us, length us, event | category | flops | bytes accessed | tf_op | source)
XLA Modules:
  0.0 580.6 jit_solution(6810668281393273272)
XLA Ops:
  6.5 1.7 copy.41
  9.0 1.0 fusion.74
  10.6 1.9 stack.8
  12.5 8.8 %all-to-all-start = ((bf16[32,128,1,2,128]{4,1,3,2,0:T(8,128)(2,1)}), bf16[32,128,1,2,128]{4,1,3,2,0:T(8,128)(2,1)S(1)}, u32[]{:S(2)}, u32[]{:S(2)}) async-start(bf16[32,128,1,2,128]{4,1,3,2,0:T(8,128)(2,1)} %stack.8), calls=%async_computation | async-start | bytes 4194304 | tf_op jit(solution)/shard_map/all_to_all | solution.py:122
  21.4 1.1 copy.42
  23.0 29.3 %all-to-all-done = bf16[32,128,1,2,128]{4,1,3,2,0:T(8,128)(2,1)S(1)} async-done(((bf16[32,128,1,2,128]{4,1,3,2,0:T(8,128)(2,1)}), bf16[32,128,1,2,128]{4,1,3,2,0:T(8,128)(2,1)S(1)}, u32[]{:S(2)}, u32[]{:S(2)}) %all-to-all-start) | async-done | bytes 2097184 | tf_op jit(solution)/shard_map/all_to_all | solution.py:122
  52.5 1.1 fusion.73
  53.6 146.2 %all-gather.3.cloned.1.call-done = bf16[16384,1,2,128]{3,0,2,1:T(8,128)(2,1)} async-done(((bf16[512,1,2,128]{3,0,2,1:T(8,128)(2,1)}), bf16[16384,1,2,128]{3,0,2,1:T(8,128)(2,1)}) %all-gather.3.cloned.1.call-update) | async-done | bytes 8388624 | tf_op jit(solution)/shard_map/all_gather | solution.py:116
  199.8 5.7 fusion.72
  205.6 126.6 %while.33 = (s32[]{:T(128)}, f32[128,1,8]{0,2,1:T(8,128)S(1)}, f32[128,1,8]{0,2,1:T(8,128)S(1)}, f32[128,1,8,128]{0,3,2,1:T(8,128)S(1)}, s32[8]{0:T(128)S(1)}, /...) while((s32[]{:T(128)}, f32[128,1,8]{0,2,1:T(8,128)S(1)}, ...), condition=%wide.region_4.5_spmd.clone, body=%wide.region_0.4_spmd.clone.sunk | while | flops 1101854720 | bytes 52800976 | solution.py:80
  207.0 5.6 bitcast_reduce_fusion.2
  212.6 5.2 fusion.100
  217.9 0.8 slice-done.1
  218.7 2.7 fusion.99
  222.8 5.6 bitcast_reduce_fusion.2
  228.4 5.2 fusion.100
  233.7 0.8 slice-done.1
  234.5 2.7 fusion.99
  238.7 5.6 bitcast_reduce_fusion.2
  244.3 5.2 fusion.100
  250.3 2.7 fusion.99
  254.5 5.6 bitcast_reduce_fusion.2
  260.1 5.2 fusion.100
  265.4 0.8 slice-done.1
  266.2 2.7 fusion.99
  270.3 5.6 bitcast_reduce_fusion.2
  275.9 5.2 fusion.100
  282.0 2.7 fusion.99
  286.1 5.6 bitcast_reduce_fusion.2
  291.8 5.2 fusion.100
  297.8 2.7 fusion.99
  302.0 5.6 bitcast_reduce_fusion.2
  307.6 5.2 fusion.100
  312.8 0.8 slice-done.1
  313.6 2.7 fusion.99
  317.8 5.6 bitcast_reduce_fusion.2
  323.4 5.2 fusion.100
  329.5 2.7 fusion.99
  332.2 14.5 %while.32 = (s32[]{:T(128)}, f32[128,1,8]{0,2,1:T(8,128)S(1)}, f32[128,1,8]{0,2,1:T(8,128)S(1)}, f32[128,1,8,128]{0,3,2,1:T(8,128)S(1)}, s32[2]{0:T(128)S(1)}, /...) while((s32[]{:T(128)}, f32[128,1,8]{0,2,1:T(8,128)S(1)}, ...), condition=%wide.region_8.9_spmd.clone, body=%wide.region_5.8_spmd.clone.sunk | while | flops 1101534336 | bytes 32851120 | solution.py:80
  333.8 1.4 fusion.91
  335.2 2.2 fusion.94
  337.4 2.0 fusion.93
  341.1 1.4 fusion.91
  342.5 2.2 fusion.94
  344.7 2.0 fusion.93
  347.8 175.1 %all-gather.5.cloned.1.call-done = bf16[4096,1024]{0,1:T(8,128)(2,1)} async-done(((bf16[128,1024]{0,1:T(8,128)(2,1)}), bf16[4096,1024]{0,1:T(8,128)(2,1)}) %all-gather.5.cloned.1.call-update) | async-done | bytes 8388624 | tf_op jit(solution)/shard_map/all_gather | solution.py:130
  522.9 7.2 %convolution_convert_fusion = bf16[4096,256]{1,0:T(8,128)(2,1)} fusion(bf16[4096,1024]{0,1:T(8,128)(2,1)} %all-gather.5.cloned.1.call-done, bf16[1024,256]{1,0:T(8,128)(2,1)S(1)} %copy-done), kind=kOutput, calls=%fused_computation.74 | convolution fusion | flops 2148532224 | bytes 11010048 | tf_op jit(solution)/shard_map/dot_general | solution.py:129
  530.1 43.9 %reduce-scatter.2.cloned.1.call-done = bf16[512,256]{1,0:T(8,128)(2,1)} async-done(((bf16[4096,256]{1,0:T(8,128)(2,1)}), bf16[512,256]{1,0:T(8,128)(2,1)}) %reduce-scatter.2.cloned.1.call-update) | async-done | bytes 262160 | tf_op jit(solution)/shard_map/reduce_scatter | solution.py:134
  (142 shorter events, 13.9 us)
Async XLA Ops:
  6.5 516.3 %copy-start = (bf16[1024,256]{1,0:T(8,128)(2,1)S(1)}, bf16[1024,256]{1,0:T(8,128)(2,1)}, u32[]{:S(2)}) copy-start(bf16[1024,256]{1,0:T(8,128)(2,1)} %param.13) | copy-start | bytes 1572868
  6.5 193.3 %all-gather.3.cloned.1.call-start = ((), (), s32[]{:S(2)}) async-start(), calls=%async_computation.2 | async-start | bytes 8650752 | tf_op jit(solution)/shard_map/all_gather | solution.py:116
  12.5 39.8 %all-to-all-start = ((bf16[32,128,1,2,128]{4,1,3,2,0:T(8,128)(2,1)}), bf16[32,128,1,2,128]{4,1,3,2,0:T(8,128)(2,1)S(1)}, u32[]{:S(2)}, u32[]{:S(2)}) async-start(bf16[32,128,1,2,128]{4,1,3,2,0:T(8,128)(2,1)} %stack.8), calls=%async_computation | async-start | bytes 4194304 | tf_op jit(solution)/shard_map/all_to_all | solution.py:122
  21.3 501.6 %all-gather.5.cloned.1.call-start = ((), (), s32[]{:S(2)}) async-start(), calls=%async_computation.3 | async-start | bytes 8650752 | tf_op jit(solution)/shard_map/all_gather | solution.py:130
  53.6 151.9 %copy-start.2 = (f32[128,1,8,128]{0,3,2,1:T(8,128)S(1)}, f32[128,1,8,128]{0,3,2,1:T(8,128)}, u32[]{:S(2)}) copy-start(f32[128,1,8,128]{0,3,2,1:T(8,128)} %custom-call.2) | copy-start | bytes 1572868
  53.6 151.9 %copy-start.3 = (s32[64]{0:T(128)S(1)}, s32[64]{0:T(128)}, u32[]{:S(2)}) copy-start(s32[64]{0:T(128)} %param.15) | copy-start | bytes 772
  212.6 5.3 slice-start
  212.6 6.1 %slice-start.1 = ((s8[8388608]{0:T(1024)(128)(4,1)}), s8[4194304]{0:T(1024)(128)(4,1)S(1)}, s32[]{:S(2)}) async-start(s8[8388608]{0:T(1024)(128)(4,1)} %bitcast.218), calls=%async_computation.6 | async-start | bytes 8388608 | tf_op jit(solution)/shard_map/while
  228.4 5.3 slice-start
  228.4 6.1 %slice-start.1 = ((s8[8388608]{0:T(1024)(128)(4,1)}), s8[4194304]{0:T(1024)(128)(4,1)S(1)}, s32[]{:S(2)}) async-start(s8[8388608]{0:T(1024)(128)(4,1)} %bitcast.218), calls=%async_computation.6 | async-start | bytes 8388608 | tf_op jit(solution)/shard_map/while
  244.2 5.3 slice-start
  244.3 6.1 %slice-start.1 = ((s8[8388608]{0:T(1024)(128)(4,1)}), s8[4194304]{0:T(1024)(128)(4,1)S(1)}, s32[]{:S(2)}) async-start(s8[8388608]{0:T(1024)(128)(4,1)} %bitcast.218), calls=%async_computation.6 | async-start | bytes 8388608 | tf_op jit(solution)/shard_map/while
  260.1 5.3 slice-start
  260.1 6.1 %slice-start.1 = ((s8[8388608]{0:T(1024)(128)(4,1)}), s8[4194304]{0:T(1024)(128)(4,1)S(1)}, s32[]{:S(2)}) async-start(s8[8388608]{0:T(1024)(128)(4,1)} %bitcast.218), calls=%async_computation.6 | async-start | bytes 8388608 | tf_op jit(solution)/shard_map/while
  275.9 5.3 slice-start
  275.9 6.1 %slice-start.1 = ((s8[8388608]{0:T(1024)(128)(4,1)}), s8[4194304]{0:T(1024)(128)(4,1)S(1)}, s32[]{:S(2)}) async-start(s8[8388608]{0:T(1024)(128)(4,1)} %bitcast.218), calls=%async_computation.6 | async-start | bytes 8388608 | tf_op jit(solution)/shard_map/while
  291.7 5.3 slice-start
  291.7 6.1 %slice-start.1 = ((s8[8388608]{0:T(1024)(128)(4,1)}), s8[4194304]{0:T(1024)(128)(4,1)S(1)}, s32[]{:S(2)}) async-start(s8[8388608]{0:T(1024)(128)(4,1)} %bitcast.218), calls=%async_computation.6 | async-start | bytes 8388608 | tf_op jit(solution)/shard_map/while
  307.6 5.3 slice-start
  307.6 6.1 %slice-start.1 = ((s8[8388608]{0:T(1024)(128)(4,1)}), s8[4194304]{0:T(1024)(128)(4,1)S(1)}, s32[]{:S(2)}) async-start(s8[8388608]{0:T(1024)(128)(4,1)} %bitcast.218), calls=%async_computation.6 | async-start | bytes 8388608 | tf_op jit(solution)/shard_map/while
  323.4 5.3 slice-start
  323.4 6.1 %slice-start.1 = ((s8[8388608]{0:T(1024)(128)(4,1)}), s8[4194304]{0:T(1024)(128)(4,1)S(1)}, s32[]{:S(2)}) async-start(s8[8388608]{0:T(1024)(128)(4,1)} %bitcast.218), calls=%async_computation.6 | async-start | bytes 8388608 | tf_op jit(solution)/shard_map/while
  332.2 3.0 copy-start.1
  339.5 3.0 copy-start.1
  347.5 226.5 %reduce-scatter.2.cloned.1.call-start = ((), (), s32[]{:S(2)}) async-start(), calls=%async_computation.4 | async-start | bytes 2359296 | tf_op jit(solution)/shard_map/reduce_scatter | solution.py:134
Sparse Core Ops, SparseCore 0:
  9.2 190.6 all-gather.2
  347.6 175.1 all-gather.4
  530.3 43.7 reduce-scatter.1
